TPU v7x, 32 devices: a whole 2x2x4 slice. The times are simulated.
32 devices in a mesh: ex: 8 (over y, x, core), feat: 4 (over z).
Axes of the slice: x: 2, y: 2, z: 4, core: 2. Of those that a mesh axis runs over, the one named last changes fastest.
Arguments:
- activations: bfloat16 [512, 64, 4096], P('ex', None, 'feat'), may hold values from -6 to 6
- output_gradient_rows: bfloat16 [512, 64, 4096], P('ex', None, 'feat'), may hold values from -6 to 6
- adapter_down_matrix: bfloat16 [4096, 128], P('feat'), may hold values from -0.09375 to 0.09375
- rank_side_sketch: bfloat16 [128, 64], replicated, may hold values from -0.5 to 0.5
- output_side_sketch: bfloat16 [4096, 128], P('feat'), may hold values from -0.09375 to 0.09375
- heldout_gradient_features: float32 [256, 8192], P('ex', 'feat'), may hold values from -6 to 6
- heldout_language_permutation: int32 [256], P('ex'), may hold values from 0 to 255, each once
Outputs:
- scores: float32 [512, 64], P('ex')
Inputs may be any that keep to these rules, and one draw needn't show every extreme that they name: `heldout_language_permutation`: every value of 0 to 255 appears once, so every language has 4 validation examples.
All inputs are finite; a program needn't handle non-finite values.
Results may differ from a plain program's by a relative error of at most 0.0029.
Values sent between devices are 32-bit elements; how exact they have to be, the bound alone decides.
No kernel may reach another device: no remote copies, remote signals or barrier semaphores. Data moves between devices by JAX's collectives and lax.ppermute only.
A program may use at most 64 MiB of HBM per device.

v0:
```python
import jax
import jax.numpy as jnp
from jax import lax
from jax.sharding import PartitionSpec as P

KF = 8192
LANGS = 64


def shards(
    activations,
    output_gradient_rows,
    adapter_down_matrix,
    rank_side_sketch,
    output_side_sketch,
    heldout_gradient_features,
    heldout_language_permutation,
):
    highest = lax.Precision.HIGHEST
    ex_dev = activations.shape[0]
    down_projection_name = jnp.dot(
        adapter_down_matrix, rank_side_sketch, preferred_element_type=jnp.float32
    ).astype(jnp.bfloat16)
    rank_part = jnp.einsum(
        "esd,dr->esr", activations, down_projection_name, preferred_element_type=jnp.float32
    )
    rank_side = lax.psum(rank_part, "feat")
    out_part = jnp.einsum(
        "esd,dk->esk", output_gradient_rows, output_side_sketch, preferred_element_type=jnp.float32
    )
    out_side = lax.psum_scatter(out_part, "feat", scatter_dimension=2, tiled=True)
    grad_feat = jnp.einsum("esk,esr->ekr", out_side, rank_side, precision=highest).reshape(
        ex_dev, -1
    )
    val_square = lax.psum(
        jnp.sum(heldout_gradient_features * heldout_gradient_features, axis=1), "feat"
    )
    val_unit = heldout_gradient_features * lax.rsqrt(val_square + 1e-06)[:, None]
    lang = heldout_language_permutation % LANGS
    onehot = (lang[:, None] == jnp.arange(LANGS, dtype=jnp.int32)[None, :]).astype(jnp.float32)
    lang_part = jnp.dot(onehot.T, val_unit, precision=highest)
    lang_mean = lax.psum(lang_part, "ex") / (
        heldout_language_permutation.shape[0] * lax.axis_size("ex") // LANGS
    )
    inner_part = jnp.dot(grad_feat, lang_mean.T, precision=highest)
    square_part = jnp.sum(grad_feat * grad_feat, axis=1)
    inner, squares = lax.psum((inner_part, square_part), "feat")
    per_lang = heldout_language_permutation.shape[0] * lax.axis_size("ex") // LANGS
    scale = jnp.sqrt(jnp.float32(KF * per_lang))
    return scale * inner * lax.rsqrt(squares + 1e-06)[:, None]


def solution(mesh):
    placed = (
        P("ex", None, "feat"),
        P("ex", None, "feat"),
        P("feat", None),
        P(),
        P("feat", None),
        P("ex", "feat"),
        P("ex"),
    )
    return jax.shard_map(
        shards, mesh=mesh, in_specs=placed, out_specs=P("ex", None), check_vma=False
    )
```

profile of v0, /device:TPU:0, one launch (start us, length us, event | category | flops | bytes accessed | tf_op | source)
XLA Modules:
  0.0 268.0 jit_solution(1419638174889042181)
XLA Ops:
  6.5 0.0 copy-start
  6.5 0.0 all-reduce.4.cloned.1.call-start
  6.5 7.4 %convolution_bitcast_fusion = f32[64,64,64]{2,1,0:T(8,128)} fusion(bf16[64,64,1024]{2,1,0:T(8,128)(2,1)} %param.7, bf16[1024,128]{1,0:T(8,128)(2,1)} %param.9, bf16[128,64]{0,1:T(8,128)(2,1)} %param.10), kind=kOutput, calls=%fused_computation | convolution fusion | flops 553713664 | bytes 9715712 | tf_op jit(solution)/shard_map/esd,dr->esr/dot_general | solution.py:24
  14.0 0.0 all-reduce.4.cloned.1.call-update
  14.0 0.0 copy-start.1
  14.0 0.0 copy-start.2
  14.0 0.0 reduce-scatter.2.cloned.1.call-start
  14.1 0.0 copy-done
  14.1 9.5 %fusion.3 = f32[64,64,128]{1,2,0:T(8,128)} fusion(bf16[64,64,1024]{2,1,0:T(8,128)(2,1)} %param.8, bf16[1024,128]{1,0:T(8,128)(2,1)S(1)} %copy-done), kind=kOutput, calls=%fused_computation.6 | convolution fusion | flops 1073741824 | bytes 10747904 | tf_op jit(solution)/shard_map/esd,dk->esk/dot_general | solution.py:28
  23.5 0.0 reduce-scatter.2.cloned.1.call-update
  23.6 0.0 all-reduce.6.cloned.1.call-start
  23.6 0.0 copy-done.1
  23.6 0.1 multiply_reduce_fusion.1
  23.7 14.1 %psum.36 = f32[32]{0:T(128)S(1)} all-reduce(f32[32]{0:T(128)S(1)} %multiply_reduce_fusion.1), channel_id=1, replica_groups=mesh['ex'=8,'feat'=4] {'feat'}, use_global_device_ids=true, to_apply=%region_3.0 | all-reduce | flops 32 | bytes 256 | tf_op jit(solution)/shard_map/psum | solution.py:35
  37.8 1.3 fusion.6
  39.1 0.0 all-reduce.6.cloned.1.call-update
  39.1 64.1 %all-reduce.4.cloned.1.call-done = f32[64,64,64]{2,1,0:T(8,128)} async-done(((f32[64,64,64]{2,1,0:T(8,128)}), f32[64,64,64]{2,1,0:T(8,128)}) %all-reduce.4.cloned.1.call-update) | async-done | bytes 1048592 | tf_op jit(solution)/shard_map/psum | solution.py:27
  103.3 78.1 %reduce-scatter.2.cloned.1.call-done = f32[64,64,32]{1,2,0:T(8,128)} async-done(((f32[64,64,128]{1,2,0:T(8,128)}), f32[64,64,32]{1,2,0:T(8,128)}) %reduce-scatter.2.cloned.1.call-update) | async-done | bytes 524304 | tf_op jit(solution)/shard_map/reduce_scatter | solution.py:31
  181.4 4.2 %multiply_reduce_fusion = (f32[64]{0:T(128)S(1)}, f32[64,32,64]{2,1,0:T(8,128)S(1)}) fusion(f32[64,64,32]{1,2,0:T(8,128)} %reduce-scatter.2.cloned.1.call-done, f32[64,64,64]{2,1,0:T(8,128)} %all-reduce.4.cloned.1.call-done), kind=kOutput, calls=%fused_computation.3 | convolution fusion | flops 100925376 | bytes 2097408 | tf_op jit(solution)/shard_map/esk,esr->ekr/dot_general | solution.py:32
  185.6 0.4 reshape.6
  186.0 53.9 %all-reduce.6.cloned.1.call-done = f32[64,2048]{1,0:T(8,128)} async-done(((f32[64,2048]{1,0:T(8,128)}), f32[64,2048]{1,0:T(8,128)}) %all-reduce.6.cloned.1.call-update) | async-done | bytes 524304 | tf_op jit(solution)/shard_map/psum | solution.py:42
  239.9 1.6 fusion.1
  241.5 19.3 %all-reduce = (f32[64,64]{1,0:T(8,128)S(1)}, f32[64]{0:T(128)S(1)}) all-reduce(f32[64,64]{1,0:T(8,128)S(1)} %fusion.1, f32[64]{0:T(128)S(1)} %get-tuple-element.7), channel_id=1, replica_groups=mesh['ex'=8,'feat'=4] {'feat'}, use_global_device_ids=true, to_apply=%region_5.6 | all-reduce | flops 4160 | bytes 33280 | tf_op jit(solution)/shard_map/psum | solution.py:47
  260.8 0.7 broadcast_multiply_fusion
  (4 shorter events, 0.0 us)
Async XLA Ops:
  6.5 7.5 %copy-start = (bf16[1024,128]{1,0:T(8,128)(2,1)S(1)}, bf16[1024,128]{1,0:T(8,128)(2,1)}, u32[]{:S(2)}) copy-start(bf16[1024,128]{1,0:T(8,128)(2,1)} %param.11) | copy-start | bytes 786436
  6.5 96.7 %all-reduce.4.cloned.1.call-start = ((), (), s32[]{:S(2)}) async-start(), calls=%async_computation.2 | async-start | bytes 4194304 | tf_op jit(solution)/shard_map/psum | solution.py:27
  14.0 9.6 %copy-start.1 = (f32[32,2048]{1,0:T(8,128)S(1)}, f32[32,2048]{1,0:T(8,128)}, u32[]{:S(2)}) copy-start(f32[32,2048]{1,0:T(8,128)} %param.12) | copy-start | bytes 786436
  14.0 23.8 %copy-start.2 = (s32[32]{0:T(128)S(1)}, s32[32]{0:T(128)}, u32[]{:S(2)}) copy-start(s32[32]{0:T(128)} %param.13) | copy-start | bytes 388
  14.0 167.4 %reduce-scatter.2.cloned.1.call-start = ((), (), s32[]{:S(2)}) async-start(), calls=%async_computation.1 | async-start | bytes 5242880 | tf_op jit(solution)/shard_map/reduce_scatter | solution.py:31
  23.6 216.3 %all-reduce.6.cloned.1.call-start = ((), (), s32[]{:S(2)}) async-start(), calls=%async_computation.3 | async-start | bytes 1048576 | tf_op jit(solution)/shard_map/psum | solution.py:42
Sparse Core Ops, SparseCore 0:
  14.1 89.1 all-reduce.3
  105.6 75.8 reduce-scatter.1
  184.5 55.3 all-reduce.5
where the time goes:
time: 268 us
  waiting for transfers between devices  196 us (73%)
  blocking collectives  33.3 us (12%)
  matrix products  23.9 us (9%)
  between operations  13.2 us (5%)
    reduce_scatter x1, waiting for transfers between devices, shards(): lax.psum_scatter(out_part, 'feat', scatter_dimension=2, tiled=True)  78.1 us
    psum x1, waiting for transfers between devices, shards(): rank_side = lax.psum(rank_part, 'feat')  64.1 us
    psum x1, waiting for transfers between devices, shards(): lax.psum(lang_part, 'ex')  53.9 us
    psum x1, blocking collectives, shards(): inner, squares = lax.psum((inner_part, square_part), 'feat')  19.3 us
    psum x1, blocking collectives, shards(): lax.psum(jnp.sum(heldout_gradient_features * heldout_gradient_features, a...  14.1 us
    dot_general x1, matrix products, shards(): jnp.einsum('esd,dk->esk', output_gradient_rows, output_side_sketch, prefe...  9.45 us
    dot_general x1, matrix products, shards(): jnp.einsum('esd,dr->esr', activations, down_projection_name, preferred_el...  7.42 us
  transfers between devices with their start and end apart: 3, of which 3 were waited for; matrix products, arithmetic and copies ran while one was open for 6% of the time, Pallas kernels for 0%

commit v1 on v0

--- a/solution.py
+++ b/solution.py
@@ -39,7 +39,7 @@
     lang = heldout_language_permutation % LANGS
     onehot = (lang[:, None] == jnp.arange(LANGS, dtype=jnp.int32)[None, :]).astype(jnp.float32)
     lang_part = jnp.dot(onehot.T, val_unit, precision=highest)
-    lang_mean = lax.psum(lang_part, "ex") / (
+    lang_mean = jnp.sum(lax.all_gather(lang_part, "ex"), axis=0) / (
         heldout_language_permutation.shape[0] * lax.axis_size("ex") // LANGS
     )
     inner_part = jnp.dot(grad_feat, lang_mean.T, precision=highest)

time: 268 us -> 217 us (0.81)
  waiting for transfers between devices: 196 us -> 141 us
    psum x1 -> x0, waiting for transfers between devices: 53.9 us -> none  [shards(): lax.psum(lang_part, 'ex')]
  transfers between devices with their start and end apart: 3 -> 3, of which waited for: 3 -> 2; matrix products, arithmetic and copies ran while one was open for 6% -> 7% of each run, Pallas kernels for 0% -> 0%
where the time goes in v1:
time: 217 us
  waiting for transfers between devices  141 us (65%)
  blocking collectives  32.8 us (15%)
  matrix products  22.9 us (11%)
  between operations  14.9 us (7%)
  other arithmetic  3.34 us (2%)
    reduce_scatter x1, waiting for transfers between devices, shards(): lax.psum_scatter(out_part, 'feat', scatter_dimension=2, tiled=True)  78.1 us
    psum x1, waiting for transfers between devices, shards(): rank_side = lax.psum(rank_part, 'feat')  63.2 us
    psum x1, blocking collectives, shards(): inner, squares = lax.psum((inner_part, square_part), 'feat')  18.6 us
    psum x1, blocking collectives, shards(): lax.psum(jnp.sum(heldout_gradient_features * heldout_gradient_features, a...  14.1 us
    dot_general x1, matrix products, shards(): jnp.einsum('esd,dk->esk', output_gradient_rows, output_side_sketch, prefe...  9.49 us
    dot_general x1, matrix products, shards(): jnp.einsum('esd,dr->esr', activations, down_projection_name, preferred_el...  7.37 us
  transfers between devices with their start and end apart: 3, of which 2 were waited for; matrix products, arithmetic and copies ran while one was open for 7% of the time, Pallas kernels for 0%

profile of v1, /device:TPU:0, one launch (start us, length us, event | category | flops | bytes accessed | tf_op | source)
XLA Modules:
  0.0 216.6 jit_solution(14766126792508833668)
XLA Ops:
  7.4 0.0 copy-start
  7.4 0.0 all-reduce.3.cloned.1.call-start
  7.4 7.4 %convolution_bitcast_fusion = f32[64,64,64]{2,1,0:T(8,128)} fusion(bf16[64,64,1024]{2,1,0:T(8,128)(2,1)} %param.7, bf16[1024,128]{1,0:T(8,128)(2,1)} %param.9, bf16[128,64]{0,1:T(8,128)(2,1)} %param.10), kind=kOutput, calls=%fused_computation | convolution fusion | flops 553713664 | bytes 9715712 | tf_op jit(solution)/shard_map/esd,dr->esr/dot_general | solution.py:24
  14.7 0.0 all-reduce.3.cloned.1.call-update
  14.8 0.0 reduce-scatter.2.cloned.1.call-start
  14.8 0.0 copy-done
  14.8 9.5 %fusion.3 = f32[64,64,128]{1,2,0:T(8,128)} fusion(bf16[64,64,1024]{2,1,0:T(8,128)(2,1)} %param.8, bf16[1024,128]{1,0:T(8,128)(2,1)S(1)} %copy-done), kind=kOutput, calls=%fused_computation.6 | convolution fusion | flops 1073741824 | bytes 10747904 | tf_op jit(solution)/shard_map/esd,dk->esk/dot_general | solution.py:28
  24.3 0.0 reduce-scatter.2.cloned.1.call-update
  24.3 0.0 all-gather.3.cloned.1.call-start
  24.4 0.9 copy-done.1
  25.3 0.1 multiply_reduce_fusion.1
  25.4 14.1 %psum.29 = f32[32]{0:T(128)S(1)} all-reduce(f32[32]{0:T(128)S(1)} %multiply_reduce_fusion.1), channel_id=1, replica_groups=mesh['ex'=8,'feat'=4] {'feat'}, use_global_device_ids=true, to_apply=%region_3.0 | all-reduce | flops 32 | bytes 256 | tf_op jit(solution)/shard_map/psum | solution.py:35
  39.5 0.0 copy-done.2
  39.6 1.3 fusion.6
  40.8 0.0 all-gather.3.cloned.1.call-update
  40.9 63.2 %all-reduce.3.cloned.1.call-done = f32[64,64,64]{2,1,0:T(8,128)} async-done(((f32[64,64,64]{2,1,0:T(8,128)}), f32[64,64,64]{2,1,0:T(8,128)}) %all-reduce.3.cloned.1.call-update) | async-done | bytes 1048592 | tf_op jit(solution)/shard_map/psum | solution.py:27
  104.1 78.1 %reduce-scatter.2.cloned.1.call-done = f32[64,64,32]{1,2,0:T(8,128)} async-done(((f32[64,64,128]{1,2,0:T(8,128)}), f32[64,64,32]{1,2,0:T(8,128)}) %reduce-scatter.2.cloned.1.call-update) | async-done | bytes 524304 | tf_op jit(solution)/shard_map/reduce_scatter | solution.py:31
  182.2 4.2 %multiply_reduce_fusion = (f32[64]{0:T(128)S(1)}, f32[64,32,64]{2,1,0:T(8,128)S(1)}) fusion(f32[64,64,32]{1,2,0:T(8,128)} %reduce-scatter.2.cloned.1.call-done, f32[64,64,64]{2,1,0:T(8,128)} %all-reduce.3.cloned.1.call-done), kind=kOutput, calls=%fused_computation.3 | convolution fusion | flops 100925376 | bytes 2097408 | tf_op jit(solution)/shard_map/esk,esr->ekr/dot_general | solution.py:32
  186.4 0.4 reshape.6
  186.7 0.0 all-gather.3.cloned.1.call-done
  186.8 2.5 %reduce_sum.28 = f32[64,2048]{1,0:T(8,128)S(1)} reduce(f32[8,64,2048]{2,1,0:T(8,128)} %bitcast.17, f32[]{:T(128)} %constant.21.clone.1), dimensions={0}, to_apply=%region_4.5 | reduce | flops 917504 | bytes 4718596 | tf_op jit(solution)/shard_map/reduce_sum | solution.py:42
  189.3 0.6 fusion.1
  189.9 18.6 %all-reduce = (f32[64,64]{1,0:T(8,128)S(1)}, f32[64]{0:T(128)S(1)}) all-reduce(f32[64,64]{1,0:T(8,128)S(1)} %fusion.1, f32[64]{0:T(128)S(1)} %get-tuple-element.7), channel_id=1, replica_groups=mesh['ex'=8,'feat'=4] {'feat'}, use_global_device_ids=true, to_apply=%region_5.6 | all-reduce | flops 4160 | bytes 33280 | tf_op jit(solution)/shard_map/psum | solution.py:47
  208.5 0.7 broadcast_multiply_fusion
  (5 shorter events, 0.0 us)
Async XLA Ops:
  7.4 7.5 %copy-start = (bf16[1024,128]{1,0:T(8,128)(2,1)S(1)}, bf16[1024,128]{1,0:T(8,128)(2,1)}, u32[]{:S(2)}) copy-start(bf16[1024,128]{1,0:T(8,128)(2,1)} %param.11) | copy-start | bytes 786436
  7.4 96.7 %all-reduce.3.cloned.1.call-start = ((), (), s32[]{:S(2)}) async-start(), calls=%async_computation.2 | async-start | bytes 4194304 | tf_op jit(solution)/shard_map/psum | solution.py:27
  14.8 167.4 %reduce-scatter.2.cloned.1.call-start = ((), (), s32[]{:S(2)}) async-start(), calls=%async_computation.1 | async-start | bytes 5242880 | tf_op jit(solution)/shard_map/reduce_scatter | solution.py:31
  24.3 0.9 copy-start.1
  24.3 15.2 %copy-start.2 = (s32[32]{0:T(128)S(1)}, s32[32]{0:T(128)}, u32[]{:S(2)}) copy-start(s32[32]{0:T(128)} %param.13) | copy-start | bytes 388
  24.3 162.4 %all-gather.3.cloned.1.call-start = ((), (), s32[]{:S(2)}) async-start(), calls=%async_computation.3 | async-start | bytes 4718592 | tf_op jit(solution)/shard_map/all_gather | solution.py:42
Sparse Core Ops, SparseCore 0:
  14.9 89.1 all-reduce.2
  106.3 75.8 reduce-scatter.1
Sparse Core Ops, SparseCore 1:
  40.9 34.6 all-gather.2
